TPU v7x, 128 devices: a whole 4x4x4 slice. The times are simulated.
128 devices in a mesh: energy: 8 (over x, y_lo), row: 4 (over z), col: 4 (over y_hi, core).
Axes of the slice: x: 4, y: 4 (y_hi: 2, y_lo: 2; y = y_hi * 2 + y_lo), z: 4, core: 2. Of those that a mesh axis runs over, the one named last changes fastest.
Arguments:
- object_field: float32 [2, 32, 1024, 1024], P(None, 'energy', 'row', 'col'), may hold values from -6 to 6
- probe_field: float32 [2, 32, 256, 256], P(None, 'energy'), may hold values from -5 to 5
- amplitudes: float32 [32, 4, 4, 4, 256, 256], P('energy', 'row', 'col'), may hold values from 0 to 3
- kk_kernel: float32 [2, 2, 32, 32], replicated, may hold values from -0.75 to 0.75
- offsets: int32 [4, 4, 4, 2], P('row', 'col'), may hold values from 0 to 128, as said below
Outputs:
- blended: float32 [2, 32, 1024, 1024], P(None, 'energy', 'row', 'col')
- new_probe: float32 [2, 32, 256, 256], P(None, 'energy')
Inputs may be any that keep to these rules, and one draw needn't show every extreme that they name: `offsets`: position k of every tile starts within 32 of 0 for k = 0, 1 and within 32 below 128 for k = 2, 3 in rows; in columns likewise, near 0 for even k and near the top for odd k.
All inputs are finite; a program needn't handle non-finite values.
Results may differ from a plain program's by a relative error of at most 0.0001.
Values sent between devices are 32-bit elements; how exact they have to be, the bound alone decides.
A program may use at most 128 MiB of HBM per device.

v0:
```python
import functools

import jax
import jax.numpy as jnp
import numpy as np
from jax import lax
from jax.experimental import pallas as pl
from jax.experimental.pallas import tpu as pltpu
from jax.sharding import PartitionSpec as P

H = 128
N = 256
HALO = 64
STEP = 0.25
PROBE_STEP = 0.5
FLOOR = 0.25
F32 = jnp.float32
BF = jnp.bfloat16
MESH = pl.DeviceIdType.MESH
SIDES = ((-1, 0), (1, 0), (0, -1), (0, 1), (-1, -1), (-1, 1), (1, -1), (1, 1))


def tables():
    n = np.arange(H)[:, None].astype(np.float64)
    k = np.arange(H)[None, :].astype(np.float64)
    out = []
    for odd in (0, 1):
        angle = -2.0 * np.pi * ((n * (2 * k + odd)) % N) / N
        re, im = np.cos(angle) / 16.0, np.sin(angle) / 16.0
        out.append(np.block([[re, im], [-im, re]]))
    right = np.stack(out)
    both = np.stack([right, np.swapaxes(right, 1, 2)])
    hi = both.astype(np.float32).astype(jnp.bfloat16)
    lo = (both - hi.astype(np.float64)).astype(np.float32).astype(jnp.bfloat16)
    order = np.zeros((N, N), np.float32)
    for lane in range(H):
        order[2 * lane, lane] = 1
        order[2 * lane + 1, H + lane] = 1
    return np.stack([hi, lo], axis=2), order.astype(jnp.bfloat16)


def split(x):
    hi = x.astype(BF)
    return hi, (x - hi.astype(F32)).astype(BF)


def dot(a, b):
    return jnp.dot(a, b, preferred_element_type=F32)


def times_table(q, tab, side, odd):
    hi, lo = tab[side, odd, 0], tab[side, odd, 1]
    return dot(
        jnp.concatenate([q[...], q[:, :N]], axis=1), jnp.concatenate([hi, hi, lo], axis=0)
    )


def table_times(tab, side, odd, q):
    hi, lo = tab[side, odd, 0], tab[side, odd, 1]
    return dot(
        jnp.concatenate([hi, hi, lo], axis=1), jnp.concatenate([q[...], q[:N, :]], axis=0)
    )


def position(k, a, b, ext, probe, amp, grad, pg, tab, order, win, exi, ra, rb, la, lb, ap, asc, opad):
    base = lax.rem(k, 2)
    s = b + HALO - H * base
    rows_at = 64
    lane = lax.broadcasted_iota(jnp.int32, (rows_at, H), 1)
    keep = lane < H - s
    for rc in range(0, N, rows_at):
        rows = pl.ds(rc, rows_at)
        w = []
        for c in (0, 1):
            t = [pltpu.roll(ext[c, base + j, pl.ds(a + rc, rows_at), :], H - s, 1) for j in range(3)]
            w.append([jnp.where(keep, t[j], t[j + 1]) for j in (0, 1)])
        x = [[None, None], [None, None]]
        for j in (0, 1):
            cols = pl.ds(j * H, H)
            pr, pi = probe[0, rows, cols], probe[1, rows, cols]
            wr, wi = w[0][j], w[1][j]
            win[0, rows, cols] = wr
            win[1, rows, cols] = wi
            x[0][j] = pr * wr - pi * wi
            x[1][j] = pr * wi + pi * wr
            exi[0, rows, cols] = x[0][j]
            exi[1, rows, cols] = x[1][j]
        for c in (0, 1):
            for q, v in ((ra, x[c][0] + x[c][1]), (rb, x[c][0] - x[c][1])):
                hi, lo = split(v)
                q[rows, pl.ds(c * H, H)] = hi
                q[rows, pl.ds(N + c * H, H)] = lo
        hi, lo = split(amp[rows, :])
        ap[rows, pl.ds(0, N)] = hi
        ap[rows, pl.ds(N, N)] = lo
    y = [times_table(ra, tab, 0, 0), times_table(rb, tab, 0, 1)]
    for pc in (0, 1):
        cols = pl.ds(pc * H, H)
        for c in (0, 1):
            t = y[pc][:H, c * H:(c + 1) * H]
            u = y[pc][H:, c * H:(c + 1) * H]
            for q, v in ((la, t + u), (lb, t - u)):
                hi, lo = split(v)
                q[pl.ds(c * H, H), cols] = hi
                q[pl.ds(N + c * H, H), cols] = lo
    amps = dot(ap[...], jnp.concatenate([order[...], order[...]], axis=0))
    asc[0] = amps[:, :H]
    asc[1] = amps[:, H:]
    z = [table_times(tab, 1, 0, la), table_times(tab, 1, 1, lb)]
    for pr, q in ((0, la), (1, lb)):
        fr, fi = z[pr][:H], z[pr][H:]
        measured = jnp.concatenate([asc[j, pl.ds(pr, H, stride=2), :] for j in (0, 1)], axis=1)
        scale = measured * lax.rsqrt(jnp.maximum(fr * fr + fi * fi, FLOOR * FLOOR))
        for c, v in ((0, fr * scale), (1, fi * scale)):
            hi, lo = split(v)
            q[pl.ds(c * H, H), :] = hi
            q[pl.ds(N + c * H, H), :] = lo
    p, q = table_times(tab, 0, 0, la), table_times(tab, 0, 1, lb)
    for half, v in ((0, p + q), (1, p - q)):
        rows = pl.ds(half * H, H)
        for pc, dst in ((0, ra), (1, rb)):
            for c in (0, 1):
                hi, lo = split(v[c * H:(c + 1) * H, pc * H:(pc + 1) * H])
                dst[rows, pl.ds(c * H, H)] = hi
                dst[rows, pl.ds(N + c * H, H)] = lo
    p, q = times_table(ra, tab, 1, 0), times_table(rb, tab, 1, 1)
    back = (p + q, p - q)
    turned = lane >= s
    for rc in range(0, N, rows_at):
        rows = pl.ds(rc, rows_at)
        step = [[None] * 2, [None] * 2]
        for j in (0, 1):
            cols = pl.ds(j * H, H)
            dr = exi[0, rows, cols] - back[j][rc:rc + rows_at, :H]
            di = exi[1, rows, cols] - back[j][rc:rc + rows_at, H:]
            pr, pi = probe[0, rows, cols], probe[1, rows, cols]
            wr, wi = win[0, rows, cols], win[1, rows, cols]
            pg[0, rows, cols] += wr * dr + wi * di
            pg[1, rows, cols] += wr * di - wi * dr
            step[0][j] = pltpu.roll(pr * dr + pi * di, s, 1)
            step[1][j] = pltpu.roll(pr * di - pi * dr, s, 1)
        for c in (0, 1):
            at = pl.ds(32 + rc, rows_at)
            opad[c, 0, at, :] = jnp.where(turned, step[c][0], 0.0)
            opad[c, 1, at, :] = jnp.where(turned, step[c][1], step[c][0])
            opad[c, 2, at, :] = jnp.where(turned, 0.0, step[c][1])
    first = 96 * lax.div(k, 2)
    start = 32 - jnp.clip(a - first, 0, 32)
    for c in (0, 1):
        for j in range(3):
            for rc in range(0, 288, 32):
                at = pl.ds(pl.multiple_of(first + rc, 32), 32)
                grad[c, base + j, at, :] += opad[c, j, pl.ds(start + rc, 32), :]


def expand_kernel(kk, kx):
    out_row = lax.broadcasted_iota(jnp.int32, (512, 32), 0)
    out_col = lax.broadcasted_iota(jnp.int32, (512, 32), 1)
    out_energy = 4 * (out_row >> 6) + ((out_row >> 3) & 3)
    in_row = lax.broadcasted_iota(jnp.int32, (32, 512), 0)
    in_col = lax.broadcasted_iota(jnp.int32, (32, 512), 1)
    in_energy = 4 * ((in_col >> 4) & 7) + (in_col >> 7)
    r = lax.broadcasted_iota(jnp.int32, (512, 512), 0)
    c = lax.broadcasted_iota(jnp.int32, (512, 512), 1)
    same = (r & 7) == (c & 7)
    one = lambda m: jnp.where(m, 1.0, 0.0).astype(BF)
    pick = [one((in_energy == in_row) & (((in_col >> 3) & 1) == b)) for b in (0, 1)]
    place = [one((out_energy == out_col) & (((out_row >> 5) & 1) == a)) for a in (0, 1)]
    parts = [[split(kk[a, b]) for b in (0, 1)] for a in (0, 1)]
    for which in (0, 1):
        total = None
        for a in (0, 1):
            row = dot(parts[a][0][which], pick[0]) + dot(parts[a][1][which], pick[1])
            term = dot(place[a], row.astype(BF))
            total = term if total is None else total + term
        kx[which] = jnp.where(same, total, 0.0).astype(BF)


def kernel(
    offs, obj_any, probe_any, amp_any, kk, tab_any, order_any,
    blended_any, new_probe_any,
    obj, probe, amp, tab, order, kx,
    halo_rows, halo_cols, halo_corners, cols_out, corners_out,
    gr_in, gc_in, gk_in, gr_out, gc_out, gk_out,
    ext, grad, stepped, gathered, acc, coupled, returned,
    pg, core_in, row_in, far_in, total,
    win, exi, ra, rb, la, lb, ap, asc, opad,
    load_sem, halo_send, halo_recv, grad_send, grad_recv,
    in_send, in_recv, out_send, out_recv,
    p_send, p_recv, store_sem,
):
    me = lax.axis_index("energy")
    row = lax.axis_index("row")
    col = lax.axis_index("col")
    rows, cols = lax.axis_size("row"), lax.axis_size("col")
    core = lax.rem(col, 2)
    partner = {"col": col + 1 - 2 * core}
    high = lax.div(col, 2)
    across = {"col": col + 2 - 4 * high}

    def peer(slot):
        dx, dy = slot // 2, slot % 2
        x, y = lax.div(me, 2), lax.rem(me, 2)
        y2 = y + dy * (1 - 2 * y)
        return lax.rem(x + dx, 4) * 2 + y2, lax.rem(x + 4 - dx, 4) * 2 + y2

    def inside(dr, dc):
        ok = None
        for d, at, n in ((dr, row, rows), (dc, col, cols)):
            if d:
                here = at > 0 if d < 0 else at < n - 1
                ok = here if ok is None else ok & here
        return ok

    loads = []
    for e in range(4):
        loads.append(pltpu.make_async_copy(obj_any.at[:, e], obj.at[e], load_sem.at[e]))
    loads.append(pltpu.make_async_copy(probe_any, probe, load_sem.at[4]))
    loads.append(pltpu.make_async_copy(tab_any, tab, load_sem.at[5]))
    loads.append(pltpu.make_async_copy(order_any, order, load_sem.at[6]))
    for e in range(4):
        loads.append(pltpu.make_async_copy(amp_any.at[e, 0, 0], amp.at[e], load_sem.at[7 + e]))
    for copy in loads:
        copy.start()

    barrier = pltpu.get_barrier_semaphore()

    def greet(device):
        pl.semaphore_signal(barrier, inc=1, device_id=device, device_id_type=MESH)

    for dr, dc in SIDES:
        @pl.when(inside(dr, dc))
        def _():
            greet({"row": row + dr, "col": col + dc})
    for slot in range(1, 8):
        greet({"energy": peer(slot)[0]})
    for d in range(1, 4):
        r2 = lax.rem(row + d, rows)

        @pl.when((r2 != row + 1) & (r2 != row - 1))
        def _():
            greet({"row": r2})
    greet(across)
    near_rows = jnp.where(row > 0, 1, 0) + jnp.where(row < rows - 1, 1, 0)
    near_cols = jnp.where(col > 0, 1, 0) + jnp.where(col < cols - 1, 1, 0)
    pl.semaphore_wait(barrier, 11 + near_cols + near_rows * near_cols)

    lane = lax.broadcasted_iota(jnp.int32, (H, H), 1)
    low = lane < 64
    lane64 = lax.broadcasted_iota(jnp.int32, (64, H), 1)
    low64 = lane64 < 64

    def fold(t, keep_low):
        first, second = t
        n = first.shape[0]
        m = low if n == H else low64
        return jnp.where(m if keep_low else ~m, first, pltpu.roll(second, 64, 1))

    def halo_copy(i, e):
        dr, dc = SIDES[i]
        to = {"row": row + dr, "col": col + dc}
        if dc == 0:
            src, dst = obj.at[e, :, pl.ds(0 if dr < 0 else N - HALO, HALO), :], halo_rows.at[i, e]
        elif dr == 0:
            src, dst = cols_out.at[i - 2, e], halo_cols.at[i - 2, e]
        else:
            src, dst = corners_out.at[i - 4, e], halo_corners.at[i - 4, e]
        return pltpu.make_async_remote_copy(
            src_ref=src, dst_ref=dst, send_sem=halo_send.at[i, e], recv_sem=halo_recv.at[i, e],
            device_id=to, device_id_type=MESH,
        )

    for e in range(4):
        loads[e].wait()
        for i, dc in ((2, -1), (3, 1)):
            at = pl.ds(0 if dc < 0 else H, H)
            for c in (0, 1):
                cols_out[i - 2, e, c] = fold((obj[e, c, :H, at], obj[e, c, H:, at]), dc < 0)
        for i in range(4, 8):
            dr, dc = SIDES[i]
            at = pl.ds(0 if dc < 0 else H, H)
            rr = pl.ds(0 if dr < 0 else N - HALO, HALO)
            corners_out[i - 4, e] = fold((obj[e, 0, rr, at], obj[e, 1, rr, at]), dc < 0)
        for i, (dr, dc) in enumerate(SIDES):
            @pl.when(inside(dr, dc))
            def _():
                halo_copy(i, e).start()

    expand_kernel(kk, kx)
    opad[:, :, :32, :] = jnp.zeros((2, 3, 32, H), F32)
    opad[:, :, 288:, :] = jnp.zeros((2, 3, 32, H), F32)
    loads[4].wait()
    loads[5].wait()
    loads[6].wait()
    pg[...] = jnp.zeros_like(pg)

    def assemble(e):
        pltpu.make_async_copy(amp_any.at[e, 0, 0], amp.at[e], load_sem.at[7 + e]).wait()
        grad[...] = jnp.zeros_like(grad)
        for c in (0, 1):
            for j in (0, 1):
                ext[c, 1 + j, pl.ds(64, N), :] = obj[e, c, :, pl.ds(j * H, H)]
        for i, (dr, dc) in enumerate(SIDES):
            rr = pl.ds(64, N) if dr == 0 else pl.ds(0 if dr > 0 else 320, 64)
            tile = 0 if dc > 0 else 3

            @pl.when(inside(-dr, -dc))
            def _():
                halo_copy(i, e).wait_recv()
                for c in (0, 1):
                    if dc == 0:
                        for j in (0, 1):
                            ext[c, 1 + j, rr, :] = halo_rows[i, e, c, :, pl.ds(j * H, H)]
                    elif dr == 0:
                        v = halo_cols[i - 2, e, c]
                        ext[c, tile, pl.ds(64, H), :] = v
                        ext[c, tile, pl.ds(64 + H, H), :] = pltpu.roll(v, 64, 1)
                    else:
                        v = halo_corners[i - 4, e]
                        ext[c, tile, rr, :] = v if c == 0 else pltpu.roll(v, 64, 1)

            @pl.when(jnp.logical_not(inside(-dr, -dc)))
            def _():
                for c in (0, 1):
                    for t in ((1, 2) if dc == 0 else (tile,)):
                        ext[c, t, rr, :] = jnp.zeros((256 if dr == 0 else 64, H), F32)

    def grad_copy(i, e):
        dr, dc = SIDES[i]
        to = {"row": row + dr, "col": col + dc}
        if dc == 0:
            src, dst = gr_out.at[i, e], gr_in.at[i, e]
        elif dr == 0:
            src, dst = gc_out.at[i - 2, e], gc_in.at[i - 2, e]
        else:
            src, dst = gk_out.at[i - 4, e], gk_in.at[i - 4, e]
        return pltpu.make_async_remote_copy(
            src_ref=src, dst_ref=dst, send_sem=grad_send.at[i, e], recv_sem=grad_recv.at[i, e],
            device_id=to, device_id_type=MESH,
        )

    def hand_over(e):
        for i, (dr, dc) in enumerate(SIDES):
            rr = pl.ds(0 if dr < 0 else 320, 64)
            tile = 0 if dc < 0 else 3

            @pl.when(inside(dr, dc))
            def _():
                if dc == 0:
                    for c in (0, 1):
                        for j in (0, 1):
                            gr_out[i, e, c, :, pl.ds(j * H, H)] = grad[c, 1 + j, rr, :]
                elif dr == 0:
                    for c in (0, 1):
                        gc_out[i - 2, e, c] = fold(
                            (grad[c, tile, pl.ds(64, H), :], grad[c, tile, pl.ds(64 + H, H), :]), dc > 0
                        )
                else:
                    gk_out[i - 4, e] = fold((grad[0, tile, rr, :], grad[1, tile, rr, :]), dc > 0)
                grad_copy(i, e).start()
        for c in (0, 1):
            for j in (0, 1):
                at = pl.ds(j * H, H)
                stepped[e, c, :, at] = obj[e, c, :, at] - STEP * grad[c, 1 + j, pl.ds(64, N), :]

    def in_copy(slot, e):
        to, _ = peer(slot)
        return pltpu.make_async_remote_copy(
            src_ref=stepped.at[e, :, pl.ds(pl.multiple_of(32 * to, 32), 32), :],
            dst_ref=gathered.at[e, me],
            send_sem=in_send.at[slot - 1, e], recv_sem=in_recv.at[slot - 1, e],
            device_id={"energy": to}, device_id_type=MESH,
        )

    def finish(e):
        for i, (dr, dc) in enumerate(SIDES):
            rr = pl.ds(0 if dr > 0 else N - HALO, HALO)
            at = pl.ds(0 if dc > 0 else H, H)

            @pl.when(inside(-dr, -dc))
            def _():
                grad_copy(i, e).wait_recv()
                for c in (0, 1):
                    if dc == 0:
                        stepped[e, c, rr, :] -= STEP * gr_in[i, e, c]
                    elif dr == 0:
                        v = gc_in[i - 2, e, c]
                        m = low if dc > 0 else ~low
                        stepped[e, c, pl.ds(0, H), at] -= STEP * jnp.where(m, v, 0.0)
                        stepped[e, c, pl.ds(H, H), at] -= STEP * jnp.where(m, pltpu.roll(v, 64, 1), 0.0)
                    else:
                        v = gk_in[i - 4, e]
                        v = v if c == 0 else pltpu.roll(v, 64, 1)
                        stepped[e, c, rr, at] -= STEP * jnp.where(low64 if dc > 0 else ~low64, v, 0.0)
        for slot in (4, 5, 2, 6, 3, 7, 1):
            in_copy(slot, e).start()
        gathered[e, me] = stepped[e, :, pl.ds(pl.multiple_of(32 * me, 32), 32), :]

    mine = 128 * core

    def p_copy(step, batch, i):
        es = pl.ds(2 * batch, 2)
        index = (0, 1, 4, 5, 8)[step] + (i - 1 if i else 0)
        if step == 0:
            theirs = pl.ds(pl.multiple_of(128 * (1 - core), 128), 128)
            src, dst, to = pg.at[es, :, theirs, :], core_in.at[batch], partner
        elif step == 1:
            r2 = lax.rem(row + i, rows)
            src = pg.at[es, :, pl.ds(pl.multiple_of(mine + 32 * r2, 32), 32), :]
            dst, to = row_in.at[batch, i - 1], {"row": r2}
        elif step == 2:
            src = pg.at[es, :, pl.ds(pl.multiple_of(mine + 32 * row, 32), 32), :]
            dst, to = far_in.at[batch], across
        elif step == 3:
            src = total.at[es, :, pl.ds(pl.multiple_of(mine + 32 * row, 32), 32), :]
            dst, to = src, {"row": lax.rem(row + i, rows)}
        else:
            src = total.at[es, :, pl.ds(pl.multiple_of(mine, 128), 128), :]
            dst, to = src, partner
        return pltpu.make_async_remote_copy(
            src_ref=src, dst_ref=dst, send_sem=p_send.at[batch, index], recv_sem=p_recv.at[batch, index],
            device_id=to, device_id_type=MESH,
        )

    def probe_step(step, batch):
        es = pl.ds(2 * batch, 2)
        chunk = pl.ds(pl.multiple_of(mine + 32 * row, 32), 32)
        if step == 0:
            p_copy(0, batch, 0).start()
        elif step == 1:
            p_copy(0, batch, 0).wait_recv()
            half = pl.ds(pl.multiple_of(mine, 128), 128)
            pg[es, :, half, :] += core_in[batch]
            for i in (2, 1, 3):
                p_copy(1, batch, i).start()
        elif step == 2:
            for i in (1, 2, 3):
                p_copy(1, batch, i).wait_recv()
            pg[es, :, chunk, :] += row_in[batch, 0] + row_in[batch, 1] + row_in[batch, 2]
            p_copy(2, batch, 0).start()
        elif step == 3:
            p_copy(2, batch, 0).wait_recv()
            total[es, :, chunk, :] = pg[es, :, chunk, :] + far_in[batch]
            for i in (2, 1, 3):
                p_copy(3, batch, i).start()
        else:
            for i in (1, 2, 3):
                p_copy(3, batch, i).wait_recv()
            p_copy(4, batch, 0).start()

    def body(t, _):
        e, k = lax.div(t, 4), lax.rem(t, 4)

        @pl.when(k == 0)
        def _():
            assemble(e)

        position(
            k, offs[0, 0, k, 0], offs[0, 0, k, 1], ext, probe.at[:, e], amp.at[e, k], grad, pg.at[e],
            tab, order, win, exi, ra, rb, la, lb, ap, asc, opad,
        )

        @pl.when(k == 3)
        def _():
            hand_over(e)

        @pl.when((k == 1) & (e > 0))
        def _():
            finish(e - 1)

        for step, when in enumerate((7, 9, 11, 13)):
            @pl.when(t == when)
            def _():
                probe_step(step, 0)
        return 0

    lax.fori_loop(0, 16, body, 0)
    probe_step(0, 1)
    probe_step(4, 0)
    probe_step(1, 1)
    finish(3)

    def half_product(g, half):
        x = gathered[pl.ds(2 * half, 2), :, :, pl.ds(8 * g, 8), :].reshape(N, N)
        hi, lo = split(x)
        k_hi, k_lo = kx[0, :, pl.ds(N * half, N)], kx[1, :, pl.ds(N * half, N)]
        return dot(
            jnp.concatenate([k_hi, k_lo, k_hi], axis=1), jnp.concatenate([hi, hi, lo], axis=0)
        )

    for e in (0, 1):
        for slot in range(1, 8):
            in_copy(slot, e).wait_recv()
    for g in range(4):
        acc[g] = half_product(g, 0)
    probe_step(2, 1)
    for e in (2, 3):
        for slot in range(1, 8):
            in_copy(slot, e).wait_recv()

    def out_copy(slot, g):
        to, _ = peer(slot)
        return pltpu.make_async_remote_copy(
            src_ref=coupled.at[to, :, :, pl.ds(8 * g, 8), :],
            dst_ref=returned.at[:, :, pl.ds(pl.multiple_of(32 * me + 8 * g, 8), 8), :],
            send_sem=out_send.at[slot - 1, g], recv_sem=out_recv.at[slot - 1, g],
            device_id={"energy": to}, device_id_type=MESH,
        )

    for g in range(4):
        out = acc[g] + half_product(g, 1)
        coupled[:, :, :, pl.ds(8 * g, 8), :] = out.reshape(8, 2, 4, 8, N)
        for slot in (4, 5, 2, 6, 3, 7, 1):
            out_copy(slot, g).start()
    own = pl.ds(pl.multiple_of(32 * me, 32), 32)
    returned[:, :, own, :] = coupled[me]
    probe_step(3, 1)
    probe_step(4, 1)
    rate = PROBE_STEP / (4 * rows * cols)
    for batch in (0, 1):
        p_copy(4, batch, 0).wait_recv()
    for e in range(4):
        for c in (0, 1):
            probe[c, e] -= rate * total[e, c]
    stores = [pltpu.make_async_copy(probe, new_probe_any, store_sem.at[0])]
    for copy in stores:
        copy.start()
    for batch in (0, 1):
        for step in range(5):
            for i in ((0,) if step in (0, 2, 4) else (1, 2, 3)):
                p_copy(step, batch, i).wait_send()
    for i, (dr, dc) in enumerate(SIDES):
        @pl.when(inside(dr, dc))
        def _():
            for e in range(4):
                halo_copy(i, e).wait_send()
                grad_copy(i, e).wait_send()
    for e in range(4):
        for slot in range(1, 8):
            in_copy(slot, e).wait_send()
    for g in range(4):
        for slot in range(1, 8):
            out_copy(slot, g).wait_recv()
    for c in (0, 1):
        for e in range(4):
            returned[c, e] += stepped[e, c]
    final = pltpu.make_async_copy(returned, blended_any, store_sem.at[1])
    final.start()
    for g in range(4):
        for slot in range(1, 8):
            out_copy(slot, g).wait_send()
    for copy in stores:
        copy.wait()
    final.wait()


def local(object_field, probe_field, amplitudes, kk_kernel, offsets):
    tab, order = tables()
    vm = lambda *shape: pltpu.VMEM(shape, F32)
    vb = lambda *shape: pltpu.VMEM(shape, BF)
    dma = pltpu.SemaphoreType.DMA
    anywhere = pl.BlockSpec(memory_space=pl.ANY)
    return pl.pallas_call(
        kernel,
        in_specs=[
            pl.BlockSpec(memory_space=pltpu.SMEM), anywhere, anywhere, anywhere,
            pl.BlockSpec(memory_space=pltpu.VMEM), anywhere, anywhere,
        ],
        out_specs=[anywhere, anywhere],
        out_shape=[
            jax.ShapeDtypeStruct(object_field.shape, F32),
            jax.ShapeDtypeStruct(probe_field.shape, F32),
        ],
        scratch_shapes=[
            vm(4, 2, N, N), vm(2, 4, N, N), vm(4, 4, N, N), vb(2, 2, 2, N, N), vb(N, N), vb(2, 512, 512),
            vm(2, 4, 2, 64, N), vm(2, 4, 2, H, H), vm(4, 4, 64, H), vm(2, 4, 2, H, H), vm(4, 4, 64, H),
            vm(2, 4, 2, 64, N), vm(2, 4, 2, H, H), vm(4, 4, 64, H),
            vm(2, 4, 2, 64, N), vm(2, 4, 2, H, H), vm(4, 4, 64, H),
            vm(2, 4, 384, H), vm(2, 4, 384, H), vm(4, 2, N, N), vm(4, 8, 2, 32, N), vm(4, 512, N),
            vm(8, 2, 4, 32, N), vm(2, 4, N, N),
            vm(4, 2, N, N), vm(2, 2, 2, H, N), vm(2, 3, 2, 2, 32, N), vm(2, 2, 2, 32, N), vm(4, 2, N, N),
            vm(2, N, N), vm(2, N, N), vb(N, 2 * N), vb(N, 2 * N), vb(2 * N, N), vb(2 * N, N),
            vb(N, 2 * N), vm(2, N, H), vm(2, 3, 320, H),
            dma((11,)), dma((8, 4)), dma((8, 4)), dma((8, 4)), dma((8, 4)),
            dma((7, 4)), dma((7, 4)), dma((7, 4)), dma((7, 4)),
            dma((2, 9)), dma((2, 9)), dma((2,)),
        ],
        compiler_params=pltpu.CompilerParams(
            collective_id=0, has_side_effects=True, vmem_limit_bytes=64 * 2**20 - 128 * 1024
        ),
        name="gradient_step",
    )(
        offsets, object_field, probe_field, amplitudes, kk_kernel,
        jnp.asarray(tab), jnp.asarray(order),
    )


def solution(mesh):
    return jax.shard_map(
        local,
        mesh=mesh,
        in_specs=(
            P(None, "energy", "row", "col"),
            P(None, "energy", None, None),
            P("energy", "row", "col", None, None, None),
            P(),
            P("row", "col", None, None),
        ),
        out_specs=(P(None, "energy", "row", "col"), P(None, "energy", None, None)),
        check_vma=False,
    )
```

profile of v0, /device:TPU:1, one launch (start us, length us, event | category | flops | bytes accessed | tf_op | source)
XLA Modules:
  0.0 112.9 jit_solution(3888970699153074625)
XLA Ops:
  0.6 1.3 %copy.9.offs = s32[1,1,4,2]{3,2,1,0:T(4,128)} copy(s32[1,1,4,2]{2,3,1,0:T(2,128)} %param.11) | data formatting | bytes 64 | tf_op args[4]
  2.0 106.4 %gradient_step.1 = (f32[2,4,256,256]{3,2,1,0:T(8,128)}, f32[2,4,256,256]{3,2,1,0:T(8,128)}) custom-call(s32[1,1,4,2]{3,2,1,0:T(4,128)} %copy.9.offs, f32[2,4,256,256]{3,2,1,0:T(8,128)} %obj_any.1, f32[2,4,256,256]{3,2,1,0:T(8,128)} %probe_any.1, f32[4,1,1,4,256,256]{5,4,3,2,1,0:T(8,128)} %amp_any.1, f32[2,2,32,32]{3,2,1,0:T(8,128)} %kk.1, ...), custom_call_target="tpu_custom_call" | custom-call | tf_op jit(solution)/shard_map/gradient_step/pallas_call | solution.py:563
  108.4 0.0 copy-start
  108.4 3.2 %copy.12 = f32[2,4,256,256]{3,2,1,0:T(8,128)} copy(f32[2,4,256,256]{3,2,1,0:T(8,128)} %get-tuple-element.4) | data formatting | bytes 4194304
  111.6 0.0 copy-done
  111.6 1.3 %copy.13 = f32[2,4,256,256]{3,2,1,0:T(8,128)} copy(f32[2,4,256,256]{3,2,1,0:T(8,128)S(1)} %copy-done) | data formatting | bytes 4194304
Async XLA Ops:
  108.4 3.2 %copy-start = (f32[2,4,256,256]{3,2,1,0:T(8,128)S(1)}, f32[2,4,256,256]{3,2,1,0:T(8,128)}, u32[]{:S(2)}) copy-start(f32[2,4,256,256]{3,2,1,0:T(8,128)} %get-tuple-element.5) | copy-start | bytes 6291460
where the time goes:
time: 113 us
  Pallas kernels  106 us (94%)
  local copies, waits for them, and re-layouts  5.85 us (5%)
    pallas_call x1, Pallas kernels, local(): pl.pallas_call(kernel, in_specs=[pl.BlockSpec(memory_space=pltpu.SMEM), a...  106 us
    unnamed x5, local copies, waits for them, and re-layouts  5.85 us

commit v1 on v0

--- a/solution.py
+++ b/solution.py
@@ -62,7 +62,7 @@
     )
 
 
-def position(k, a, b, ext, probe, amp, grad, pg, tab, order, win, exi, ra, rb, la, lb, ap, asc, opad):
+def forward(k, a, b, ext, probe, amp, tab, order, win, exi, ra, rb, la, lb, ap, asc, opad):
     base = lax.rem(k, 2)
     s = b + HALO - H * base
     rows_at = 64
@@ -93,7 +93,10 @@
         hi, lo = split(amp[rows, :])
         ap[rows, pl.ds(0, N)] = hi
         ap[rows, pl.ds(N, N)] = lo
+    yield
     y = [times_table(ra, tab, 0, 0), times_table(rb, tab, 0, 1)]
+    amps = dot(ap[...], jnp.concatenate([order[...], order[...]], axis=0))
+    yield
     for pc in (0, 1):
         cols = pl.ds(pc * H, H)
         for c in (0, 1):
@@ -103,10 +106,11 @@
                 hi, lo = split(v)
                 q[pl.ds(c * H, H), cols] = hi
                 q[pl.ds(N + c * H, H), cols] = lo
-    amps = dot(ap[...], jnp.concatenate([order[...], order[...]], axis=0))
     asc[0] = amps[:, :H]
     asc[1] = amps[:, H:]
+    yield
     z = [table_times(tab, 1, 0, la), table_times(tab, 1, 1, lb)]
+    yield
     for pr, q in ((0, la), (1, lb)):
         fr, fi = z[pr][:H], z[pr][H:]
         measured = jnp.concatenate([asc[j, pl.ds(pr, H, stride=2), :] for j in (0, 1)], axis=1)
@@ -115,7 +119,16 @@
             hi, lo = split(v)
             q[pl.ds(c * H, H), :] = hi
             q[pl.ds(N + c * H, H), :] = lo
+    yield
+
+
+def backward(k, a, b, probe, grad, pg, tab, win, exi, ra, rb, la, lb, ap, asc, opad):
+    base = lax.rem(k, 2)
+    s = b + HALO - H * base
+    rows_at = 64
+    lane = lax.broadcasted_iota(jnp.int32, (rows_at, H), 1)
     p, q = table_times(tab, 0, 0, la), table_times(tab, 0, 1, lb)
+    yield
     for half, v in ((0, p + q), (1, p - q)):
         rows = pl.ds(half * H, H)
         for pc, dst in ((0, ra), (1, rb)):
@@ -123,7 +136,9 @@
                 hi, lo = split(v[c * H:(c + 1) * H, pc * H:(pc + 1) * H])
                 dst[rows, pl.ds(c * H, H)] = hi
                 dst[rows, pl.ds(N + c * H, H)] = lo
+    yield
     p, q = times_table(ra, tab, 1, 0), times_table(rb, tab, 1, 1)
+    yield
     back = (p + q, p - q)
     turned = lane >= s
     for rc in range(0, N, rows_at):
@@ -144,6 +159,7 @@
             opad[c, 0, at, :] = jnp.where(turned, step[c][0], 0.0)
             opad[c, 1, at, :] = jnp.where(turned, step[c][1], step[c][0])
             opad[c, 2, at, :] = jnp.where(turned, 0.0, step[c][1])
+    yield
     first = 96 * lax.div(k, 2)
     start = 32 - jnp.clip(a - first, 0, 32)
     for c in (0, 1):
@@ -151,6 +167,18 @@
             for rc in range(0, 288, 32):
                 at = pl.ds(pl.multiple_of(first + rc, 32), 32)
                 grad[c, base + j, at, :] += opad[c, j, pl.ds(start + rc, 32), :]
+    yield
+
+
+ORDER = "frfrrffrrf"
+
+
+def together(order, back, forth=None):
+    for which in order:
+        if which == "r":
+            next(back)
+        elif forth is not None:
+            next(forth)
 
 
 def expand_kernel(kk, kx):
@@ -178,17 +206,17 @@
 
 def kernel(
     offs, obj_any, probe_any, amp_any, kk, tab_any, order_any,
-    blended_any, new_probe_any,
+    blended, new_probe,
     obj, probe, amp, tab, order, kx,
     halo_rows, halo_cols, halo_corners, cols_out, corners_out,
     gr_in, gc_in, gk_in, gr_out, gc_out, gk_out,
     ext, grad, stepped, gathered, acc, coupled, returned,
     pg, core_in, row_in, far_in, total,
-    win, exi, ra, rb, la, lb, ap, asc, opad,
     load_sem, halo_send, halo_recv, grad_send, grad_recv,
-    in_send, in_recv, out_send, out_recv,
-    p_send, p_recv, store_sem,
+    in_send, in_recv, out_send, out_recv, p_send, p_recv,
+    *work,
 ):
+    work_a, work_b = work[:9], work[9:]
     me = lax.axis_index("energy")
     row = lax.axis_index("row")
     col = lax.axis_index("col")
@@ -287,8 +315,13 @@
                 halo_copy(i, e).start()
 
     expand_kernel(kk, kx)
-    opad[:, :, :32, :] = jnp.zeros((2, 3, 32, H), F32)
-    opad[:, :, 288:, :] = jnp.zeros((2, 3, 32, H), F32)
+    for buffers in (work_a, work_b):
+        opad = buffers[8]
+        opad[:, :, :32, :] = jnp.zeros((2, 3, 32, H), F32)
+        opad[:, :, 288:, :] = jnp.zeros((2, 3, 32, H), F32)
+    for part in (0, 1, 4, 5):
+        work_b[part][...] = jnp.zeros_like(work_b[part])
+    grad[...] = jnp.zeros_like(grad)
     loads[4].wait()
     loads[5].wait()
     loads[6].wait()
@@ -296,7 +329,6 @@
 
     def assemble(e):
         pltpu.make_async_copy(amp_any.at[e, 0, 0], amp.at[e], load_sem.at[7 + e]).wait()
-        grad[...] = jnp.zeros_like(grad)
         for c in (0, 1):
             for j in (0, 1):
                 ext[c, 1 + j, pl.ds(64, N), :] = obj[e, c, :, pl.ds(j * H, H)]
@@ -398,87 +430,100 @@
 
     mine = 128 * core
 
-    def p_copy(step, batch, i):
-        es = pl.ds(2 * batch, 2)
+    def p_copy(step, e, i):
         index = (0, 1, 4, 5, 8)[step] + (i - 1 if i else 0)
         if step == 0:
             theirs = pl.ds(pl.multiple_of(128 * (1 - core), 128), 128)
-            src, dst, to = pg.at[es, :, theirs, :], core_in.at[batch], partner
+            src, dst, to = pg.at[e, :, theirs, :], core_in.at[e], partner
         elif step == 1:
             r2 = lax.rem(row + i, rows)
-            src = pg.at[es, :, pl.ds(pl.multiple_of(mine + 32 * r2, 32), 32), :]
-            dst, to = row_in.at[batch, i - 1], {"row": r2}
+            src = pg.at[e, :, pl.ds(pl.multiple_of(mine + 32 * r2, 32), 32), :]
+            dst, to = row_in.at[e, i - 1], {"row": r2}
         elif step == 2:
-            src = pg.at[es, :, pl.ds(pl.multiple_of(mine + 32 * row, 32), 32), :]
-            dst, to = far_in.at[batch], across
+            src = pg.at[e, :, pl.ds(pl.multiple_of(mine + 32 * row, 32), 32), :]
+            dst, to = far_in.at[e], across
         elif step == 3:
-            src = total.at[es, :, pl.ds(pl.multiple_of(mine + 32 * row, 32), 32), :]
+            src = total.at[e, :, pl.ds(pl.multiple_of(mine + 32 * row, 32), 32), :]
             dst, to = src, {"row": lax.rem(row + i, rows)}
         else:
-            src = total.at[es, :, pl.ds(pl.multiple_of(mine, 128), 128), :]
+            src = total.at[e, :, pl.ds(pl.multiple_of(mine, 128), 128), :]
             dst, to = src, partner
         return pltpu.make_async_remote_copy(
-            src_ref=src, dst_ref=dst, send_sem=p_send.at[batch, index], recv_sem=p_recv.at[batch, index],
+            src_ref=src, dst_ref=dst, send_sem=p_send.at[e, index], recv_sem=p_recv.at[e, index],
             device_id=to, device_id_type=MESH,
         )
 
-    def probe_step(step, batch):
-        es = pl.ds(2 * batch, 2)
+    def probe_step(step, e):
         chunk = pl.ds(pl.multiple_of(mine + 32 * row, 32), 32)
         if step == 0:
-            p_copy(0, batch, 0).start()
+            p_copy(0, e, 0).start()
         elif step == 1:
-            p_copy(0, batch, 0).wait_recv()
+            p_copy(0, e, 0).wait_recv()
             half = pl.ds(pl.multiple_of(mine, 128), 128)
-            pg[es, :, half, :] += core_in[batch]
+            pg[e, :, half, :] += core_in[e]
             for i in (2, 1, 3):
-                p_copy(1, batch, i).start()
+                p_copy(1, e, i).start()
         elif step == 2:
             for i in (1, 2, 3):
-                p_copy(1, batch, i).wait_recv()
-            pg[es, :, chunk, :] += row_in[batch, 0] + row_in[batch, 1] + row_in[batch, 2]
-            p_copy(2, batch, 0).start()
+                p_copy(1, e, i).wait_recv()
+            pg[e, :, chunk, :] += row_in[e, 0] + row_in[e, 1] + row_in[e, 2]
+            p_copy(2, e, 0).start()
         elif step == 3:
-            p_copy(2, batch, 0).wait_recv()
-            total[es, :, chunk, :] = pg[es, :, chunk, :] + far_in[batch]
+            p_copy(2, e, 0).wait_recv()
+            total[e, :, chunk, :] = pg[e, :, chunk, :] + far_in[e]
             for i in (2, 1, 3):
-                p_copy(3, batch, i).start()
+                p_copy(3, e, i).start()
         else:
             for i in (1, 2, 3):
-                p_copy(3, batch, i).wait_recv()
-            p_copy(4, batch, 0).start()
+                p_copy(3, e, i).wait_recv()
+            p_copy(4, e, 0).start()
+
+    def front(k, e, buffers):
+        return forward(
+            k, offs[0, 0, 0, k], offs[0, 0, 1, k], ext, probe.at[:, e], amp.at[e, k], tab, order, *buffers
+        )
+
+    def rear(k, e, buffers):
+        return backward(
+            k, offs[0, 0, 0, k], offs[0, 0, 1, k], probe.at[:, e], grad, pg.at[e], tab, *buffers
+        )
 
     def body(t, _):
-        e, k = lax.div(t, 4), lax.rem(t, 4)
-
-        @pl.when(k == 0)
+        e, odd = lax.div(t, 2), lax.rem(t, 2)
+
+        @pl.when(odd == 0)
         def _():
             assemble(e)
 
-        position(
-            k, offs[0, 0, k, 0], offs[0, 0, k, 1], ext, probe.at[:, e], amp.at[e, k], grad, pg.at[e],
-            tab, order, win, exi, ra, rb, la, lb, ap, asc, opad,
-        )
-
-        @pl.when(k == 3)
+        last = jnp.maximum(lax.div(2 * t - 1, 4), 0)
+        together(ORDER, rear(3 - 2 * odd, last, work_b), front(2 * odd, e, work_a))
+
+        @pl.when((odd == 0) & (e > 0))
         def _():
-            hand_over(e)
-
-        @pl.when((k == 1) & (e > 0))
+            hand_over(e - 1)
+            grad[...] = jnp.zeros_like(grad)
+
+        @pl.when((odd == 0) & (e > 1))
         def _():
-            finish(e - 1)
-
-        for step, when in enumerate((7, 9, 11, 13)):
-            @pl.when(t == when)
+            finish(e - 2)
+
+        for step in range(3):
+            @pl.when((odd == 0) & (e > step))
             def _():
-                probe_step(step, 0)
+                probe_step(step, e - 1 - step)
+
+        together(ORDER, rear(2 * odd, e, work_a), front(2 * odd + 1, e, work_b))
         return 0
 
-    lax.fori_loop(0, 16, body, 0)
-    probe_step(0, 1)
-    probe_step(4, 0)
-    probe_step(1, 1)
+    lax.fori_loop(0, 8, body, 0)
+    together(ORDER, rear(3, 3, work_b))
+    hand_over(3)
+    finish(2)
+    for step in range(3):
+        probe_step(step, 3 - step)
     finish(3)
+    for step in (1, 2):
+        probe_step(step, 4 - step)
 
     def half_product(g, half):
         x = gathered[pl.ds(2 * half, 2), :, :, pl.ds(8 * g, 8), :].reshape(N, N)
@@ -493,16 +538,17 @@
             in_copy(slot, e).wait_recv()
     for g in range(4):
         acc[g] = half_product(g, 0)
-    probe_step(2, 1)
     for e in (2, 3):
         for slot in range(1, 8):
             in_copy(slot, e).wait_recv()
+
+    probe_step(2, 3)
 
     def out_copy(slot, g):
         to, _ = peer(slot)
         return pltpu.make_async_remote_copy(
             src_ref=coupled.at[to, :, :, pl.ds(8 * g, 8), :],
-            dst_ref=returned.at[:, :, pl.ds(pl.multiple_of(32 * me + 8 * g, 8), 8), :],
+            dst_ref=returned.at[:, :, me, pl.ds(8 * g, 8), :],
             send_sem=out_send.at[slot - 1, g], recv_sem=out_recv.at[slot - 1, g],
             device_id={"energy": to}, device_id_type=MESH,
         )
@@ -512,46 +558,38 @@
         coupled[:, :, :, pl.ds(8 * g, 8), :] = out.reshape(8, 2, 4, 8, N)
         for slot in (4, 5, 2, 6, 3, 7, 1):
             out_copy(slot, g).start()
-    own = pl.ds(pl.multiple_of(32 * me, 32), 32)
-    returned[:, :, own, :] = coupled[me]
-    probe_step(3, 1)
-    probe_step(4, 1)
+    returned[:, :, me] = coupled[me]
+    for step in (3, 4):
+        for e in range(4):
+            probe_step(step, e)
     rate = PROBE_STEP / (4 * rows * cols)
-    for batch in (0, 1):
-        p_copy(4, batch, 0).wait_recv()
     for e in range(4):
-        for c in (0, 1):
-            probe[c, e] -= rate * total[e, c]
-    stores = [pltpu.make_async_copy(probe, new_probe_any, store_sem.at[0])]
-    for copy in stores:
-        copy.start()
-    for batch in (0, 1):
+        p_copy(4, e, 0).wait_recv()
+        for c in (0, 1):
+            new_probe[c, e] = probe[c, e] - rate * total[e, c]
+    for e in range(4):
         for step in range(5):
             for i in ((0,) if step in (0, 2, 4) else (1, 2, 3)):
-                p_copy(step, batch, i).wait_send()
+                p_copy(step, e, i).wait_send()
+        for slot in range(1, 8):
+            in_copy(slot, e).wait_send()
     for i, (dr, dc) in enumerate(SIDES):
         @pl.when(inside(dr, dc))
         def _():
             for e in range(4):
                 halo_copy(i, e).wait_send()
                 grad_copy(i, e).wait_send()
-    for e in range(4):
-        for slot in range(1, 8):
-            in_copy(slot, e).wait_send()
     for g in range(4):
         for slot in range(1, 8):
             out_copy(slot, g).wait_recv()
-    for c in (0, 1):
-        for e in range(4):
-            returned[c, e] += stepped[e, c]
-    final = pltpu.make_async_copy(returned, blended_any, store_sem.at[1])
-    final.start()
+        for c in (0, 1):
+            for e in range(4):
+                for d in range(8):
+                    at = pl.ds(32 * d + 8 * g, 8)
+                    blended[c, e, at, :] = stepped[e, c, at, :] + returned[c, e, d, pl.ds(8 * g, 8), :]
     for g in range(4):
         for slot in range(1, 8):
             out_copy(slot, g).wait_send()
-    for copy in stores:
-        copy.wait()
-    final.wait()
 
 
 def local(object_field, probe_field, amplitudes, kk_kernel, offsets):
@@ -566,31 +604,28 @@
             pl.BlockSpec(memory_space=pltpu.SMEM), anywhere, anywhere, anywhere,
             pl.BlockSpec(memory_space=pltpu.VMEM), anywhere, anywhere,
         ],
-        out_specs=[anywhere, anywhere],
-        out_shape=[
-            jax.ShapeDtypeStruct(object_field.shape, F32),
-            jax.ShapeDtypeStruct(probe_field.shape, F32),
-        ],
+        out_specs=[pl.BlockSpec(memory_space=pltpu.VMEM)] * 2,
+        out_shape=[pltpu.VMEM(object_field.shape, F32), pltpu.VMEM(probe_field.shape, F32)],
         scratch_shapes=[
             vm(4, 2, N, N), vm(2, 4, N, N), vm(4, 4, N, N), vb(2, 2, 2, N, N), vb(N, N), vb(2, 512, 512),
             vm(2, 4, 2, 64, N), vm(2, 4, 2, H, H), vm(4, 4, 64, H), vm(2, 4, 2, H, H), vm(4, 4, 64, H),
             vm(2, 4, 2, 64, N), vm(2, 4, 2, H, H), vm(4, 4, 64, H),
             vm(2, 4, 2, 64, N), vm(2, 4, 2, H, H), vm(4, 4, 64, H),
             vm(2, 4, 384, H), vm(2, 4, 384, H), vm(4, 2, N, N), vm(4, 8, 2, 32, N), vm(4, 512, N),
-            vm(8, 2, 4, 32, N), vm(2, 4, N, N),
-            vm(4, 2, N, N), vm(2, 2, 2, H, N), vm(2, 3, 2, 2, 32, N), vm(2, 2, 2, 32, N), vm(4, 2, N, N),
+            vm(8, 2, 4, 32, N), vm(2, 4, 8, 32, N),
+            vm(4, 2, N, N), vm(4, 2, H, N), vm(4, 3, 2, 32, N), vm(4, 2, 32, N), vm(4, 2, N, N),
+            dma((11,)), dma((8, 4)), dma((8, 4)), dma((8, 4)), dma((8, 4)),
+            dma((7, 4)), dma((7, 4)), dma((7, 4)), dma((7, 4)), dma((4, 9)), dma((4, 9)),
+        ] + 2 * [
             vm(2, N, N), vm(2, N, N), vb(N, 2 * N), vb(N, 2 * N), vb(2 * N, N), vb(2 * N, N),
             vb(N, 2 * N), vm(2, N, H), vm(2, 3, 320, H),
-            dma((11,)), dma((8, 4)), dma((8, 4)), dma((8, 4)), dma((8, 4)),
-            dma((7, 4)), dma((7, 4)), dma((7, 4)), dma((7, 4)),
-            dma((2, 9)), dma((2, 9)), dma((2,)),
         ],
         compiler_params=pltpu.CompilerParams(
-            collective_id=0, has_side_effects=True, vmem_limit_bytes=64 * 2**20 - 128 * 1024
+            collective_id=0, has_side_effects=True, vmem_limit_bytes=56 * 2**20
         ),
         name="gradient_step",
     )(
-        offsets, object_field, probe_field, amplitudes, kk_kernel,
+        jnp.swapaxes(offsets, 2, 3), object_field, probe_field, amplitudes, kk_kernel,
         jnp.asarray(tab), jnp.asarray(order),
     )
 

time: 113 us -> 102 us (0.903)
  Pallas kernels: 106 us -> 99.1 us
  local copies, waits for them, and re-layouts: 5.85 us -> 2.64 us
    pallas_call x1, Pallas kernels: 106 us -> 99.1 us  [local(): pl.pallas_call(kernel, in_specs=[pl.BlockSpec(memory_space=pltpu.SMEM), a...]
    unnamed x5 -> x2, local copies, waits for them, and re-layouts: 5.85 us -> 2.64 us
where the time goes in v1:
time: 102 us
  Pallas kernels  99.1 us (97%)
  local copies, waits for them, and re-layouts  2.64 us (3%)
    pallas_call x1, Pallas kernels, local(): pl.pallas_call(kernel, in_specs=[pl.BlockSpec(memory_space=pltpu.SMEM), a...  99.1 us
    unnamed x2, local copies, waits for them, and re-layouts  2.64 us

profile of v1, /device:TPU:1, one launch (start us, length us, event | category | flops | bytes accessed | tf_op | source)
XLA Modules:
  0.0 102.3 jit_solution(2979743582590583006)
XLA Ops:
  0.6 99.1 %gradient_step.1 = (f32[2,4,256,256]{3,2,1,0:T(8,128)S(1)}, f32[2,4,256,256]{3,2,1,0:T(8,128)S(1)}) custom-call(s32[1,1,2,4]{3,2,1,0:T(2,128)} %bitcast.1, f32[2,4,256,256]{3,2,1,0:T(8,128)} %obj_any.1, f32[2,4,256,256]{3,2,1,0:T(8,128)} %probe_any.1, f32[4,1,1,4,256,256]{5,4,3,2,1,0:T(8,128)} %amp_any.1, f32[2,2,32,32]{3,2,1,0:T(8,128)} %kk.1, ...), custom_call_target="tpu_custom_call" | custom-call | tf_op jit(solution)/shard_map/gradient_step/pallas_call | solution.py:601
  99.7 1.3 %copy.11 = f32[2,4,256,256]{3,2,1,0:T(8,128)} copy(f32[2,4,256,256]{3,2,1,0:T(8,128)S(1)} %get-tuple-element.2) | data formatting | bytes 4194304
  101.0 1.3 %copy.12 = f32[2,4,256,256]{3,2,1,0:T(8,128)} copy(f32[2,4,256,256]{3,2,1,0:T(8,128)S(1)} %get-tuple-element.3) | data formatting | bytes 4194304

commit v2 on v1

--- a/solution.py
+++ b/solution.py
@@ -491,6 +491,10 @@
     def body(t, _):
         e, odd = lax.div(t, 2), lax.rem(t, 2)
 
+        @pl.when((odd == 0) & (e > 1))
+        def _():
+            finish(e - 2)
+
         @pl.when(odd == 0)
         def _():
             assemble(e)
@@ -502,28 +506,29 @@
         def _():
             hand_over(e - 1)
             grad[...] = jnp.zeros_like(grad)
-
-        @pl.when((odd == 0) & (e > 1))
-        def _():
-            finish(e - 2)
-
-        for step in range(3):
-            @pl.when((odd == 0) & (e > step))
-            def _():
-                probe_step(step, e - 1 - step)
+            probe_step(0, e - 1)
+
+        @pl.when((odd == 1) & (e > 0))
+        def _():
+            probe_step(1, e - 1)
+
+        @pl.when((odd == 1) & (e > 1))
+        def _():
+            probe_step(2, e - 2)
 
         together(ORDER, rear(2 * odd, e, work_a), front(2 * odd + 1, e, work_b))
         return 0
 
     lax.fori_loop(0, 8, body, 0)
+    finish(2)
     together(ORDER, rear(3, 3, work_b))
     hand_over(3)
-    finish(2)
-    for step in range(3):
-        probe_step(step, 3 - step)
+    probe_step(0, 3)
+    probe_step(1, 3)
+    probe_step(2, 2)
     finish(3)
-    for step in (1, 2):
-        probe_step(step, 4 - step)
+    probe_step(3, 0)
+    probe_step(3, 1)
 
     def half_product(g, half):
         x = gathered[pl.ds(2 * half, 2), :, :, pl.ds(8 * g, 8), :].reshape(N, N)
@@ -559,9 +564,8 @@
         for slot in (4, 5, 2, 6, 3, 7, 1):
             out_copy(slot, g).start()
     returned[:, :, me] = coupled[me]
-    for step in (3, 4):
-        for e in range(4):
-            probe_step(step, e)
+    for step, e in ((3, 2), (3, 3), (4, 0), (4, 1), (4, 2), (4, 3)):
+        probe_step(step, e)
     rate = PROBE_STEP / (4 * rows * cols)
     for e in range(4):
         p_copy(4, e, 0).wait_recv()

time: 102 us -> 103 us (level)
  the two profiles are of different devices: /device:TPU:1 before, /device:TPU:41 now
where the time goes in v2:
time: 103 us; the launch traced here: 102 us
  Pallas kernels  99 us (96%)
  local copies, waits for them, and re-layouts  2.64 us (3%)
    pallas_call x1, Pallas kernels, local(): pl.pallas_call(kernel, in_specs=[pl.BlockSpec(memory_space=pltpu.SMEM), a...  99 us
    unnamed x2, local copies, waits for them, and re-layouts  2.64 us

profile of v2, /device:TPU:41, one launch (start us, length us, event | category | flops | bytes accessed | tf_op | source)
XLA Modules:
  0.0 102.3 jit_solution(5960636904046504780)
XLA Ops:
  0.6 99.0 %gradient_step.1 = (f32[2,4,256,256]{3,2,1,0:T(8,128)S(1)}, f32[2,4,256,256]{3,2,1,0:T(8,128)S(1)}) custom-call(s32[1,1,2,4]{3,2,1,0:T(2,128)} %bitcast.1, f32[2,4,256,256]{3,2,1,0:T(8,128)} %obj_any.1, f32[2,4,256,256]{3,2,1,0:T(8,128)} %probe_any.1, f32[4,1,1,4,256,256]{5,4,3,2,1,0:T(8,128)} %amp_any.1, f32[2,2,32,32]{3,2,1,0:T(8,128)} %kk.1, ...), custom_call_target="tpu_custom_call" | custom-call | tf_op jit(solution)/shard_map/gradient_step/pallas_call | solution.py:605
  99.6 1.3 %copy.11 = f32[2,4,256,256]{3,2,1,0:T(8,128)} copy(f32[2,4,256,256]{3,2,1,0:T(8,128)S(1)} %get-tuple-element.2) | data formatting | bytes 4194304
  100.9 1.3 %copy.12 = f32[2,4,256,256]{3,2,1,0:T(8,128)} copy(f32[2,4,256,256]{3,2,1,0:T(8,128)S(1)} %get-tuple-element.3) | data formatting | bytes 4194304

commit v3 on v1

--- a/solution.py
+++ b/solution.py
@@ -213,7 +213,7 @@
     ext, grad, stepped, gathered, acc, coupled, returned,
     pg, core_in, row_in, far_in, total,
     load_sem, halo_send, halo_recv, grad_send, grad_recv,
-    in_send, in_recv, out_send, out_recv, p_send, p_recv,
+    in_send, in_recv, last_send, last_recv, out_send, out_recv, p_send, p_recv,
     *work,
 ):
     work_a, work_b = work[:9], work[9:]
@@ -404,8 +404,18 @@
             device_id={"energy": to}, device_id_type=MESH,
         )
 
-    def finish(e):
-        for i, (dr, dc) in enumerate(SIDES):
+    def last_copy(slot, g):
+        to, _ = peer(slot)
+        return pltpu.make_async_remote_copy(
+            src_ref=stepped.at[3, :, pl.ds(pl.multiple_of(32 * to + 8 * g, 8), 8), :],
+            dst_ref=gathered.at[3, me, :, pl.ds(8 * g, 8), :],
+            send_sem=last_send.at[slot - 1, g], recv_sem=last_recv.at[slot - 1, g],
+            device_id={"energy": to}, device_id_type=MESH,
+        )
+
+    def receive_grad(e, sides):
+        for i in sides:
+            dr, dc = SIDES[i]
             rr = pl.ds(0 if dr > 0 else N - HALO, HALO)
             at = pl.ds(0 if dc > 0 else H, H)
 
@@ -424,6 +434,9 @@
                         v = gk_in[i - 4, e]
                         v = v if c == 0 else pltpu.roll(v, 64, 1)
                         stepped[e, c, rr, at] -= STEP * jnp.where(low64 if dc > 0 else ~low64, v, 0.0)
+
+    def finish(e):
+        receive_grad(e, range(8))
         for slot in (4, 5, 2, 6, 3, 7, 1):
             in_copy(slot, e).start()
         gathered[e, me] = stepped[e, :, pl.ds(pl.multiple_of(32 * me, 32), 32), :]
@@ -521,7 +534,19 @@
     finish(2)
     for step in range(3):
         probe_step(step, 3 - step)
-    finish(3)
+    receive_grad(3, (2, 3))
+    for first in (True, False):
+        if not first:
+            receive_grad(3, (0, 1, 4, 5, 6, 7))
+        for g in range(4):
+            for slot in (4, 5, 2, 6, 3, 7, 1):
+                to = peer(slot)[0]
+                inner = (to >= 2) & (to <= 5)
+
+                @pl.when(inner if first else jnp.logical_not(inner))
+                def _():
+                    last_copy(slot, g).start()
+    gathered[3, me] = stepped[3, :, pl.ds(pl.multiple_of(32 * me, 32), 32), :]
     for step in (1, 2):
         probe_step(step, 4 - step)
 
@@ -538,11 +563,8 @@
             in_copy(slot, e).wait_recv()
     for g in range(4):
         acc[g] = half_product(g, 0)
-    for e in (2, 3):
-        for slot in range(1, 8):
-            in_copy(slot, e).wait_recv()
-
-    probe_step(2, 3)
+    for slot in range(1, 8):
+        in_copy(slot, 2).wait_recv()
 
     def out_copy(slot, g):
         to, _ = peer(slot)
@@ -554,6 +576,10 @@
         )
 
     for g in range(4):
+        for slot in range(1, 8):
+            last_copy(slot, g).wait_recv()
+        if g == 1:
+            probe_step(2, 3)
         out = acc[g] + half_product(g, 1)
         coupled[:, :, :, pl.ds(8 * g, 8), :] = out.reshape(8, 2, 4, 8, N)
         for slot in (4, 5, 2, 6, 3, 7, 1):
@@ -572,7 +598,9 @@
             for i in ((0,) if step in (0, 2, 4) else (1, 2, 3)):
                 p_copy(step, e, i).wait_send()
         for slot in range(1, 8):
-            in_copy(slot, e).wait_send()
+            if e < 3:
+                in_copy(slot, e).wait_send()
+            last_copy(slot, e).wait_send()
     for i, (dr, dc) in enumerate(SIDES):
         @pl.when(inside(dr, dc))
         def _():
@@ -615,7 +643,7 @@
             vm(8, 2, 4, 32, N), vm(2, 4, 8, 32, N),
             vm(4, 2, N, N), vm(4, 2, H, N), vm(4, 3, 2, 32, N), vm(4, 2, 32, N), vm(4, 2, N, N),
             dma((11,)), dma((8, 4)), dma((8, 4)), dma((8, 4)), dma((8, 4)),
-            dma((7, 4)), dma((7, 4)), dma((7, 4)), dma((7, 4)), dma((4, 9)), dma((4, 9)),
+            dma((7, 3)), dma((7, 3)), dma((7, 4)), dma((7, 4)), dma((7, 4)), dma((7, 4)), dma((4, 9)), dma((4, 9)),
         ] + 2 * [
             vm(2, N, N), vm(2, N, N), vb(N, 2 * N), vb(N, 2 * N), vb(2 * N, N), vb(2 * N, N),
             vb(N, 2 * N), vm(2, N, H), vm(2, 3, 320, H),

time: 102 us -> 99.5 us (0.975)
  Pallas kernels: 99.1 us -> 96 us
    pallas_call x1, Pallas kernels: 99.1 us -> 96 us  [local(): pl.pallas_call(kernel, in_specs=[pl.BlockSpec(memory_space=pltpu.SMEM), a...]
where the time goes in v3:
time: 99.5 us; the launch traced here: 99.3 us
  Pallas kernels  96 us (96%)
  local copies, waits for them, and re-layouts  2.64 us (3%)
    pallas_call x1, Pallas kernels, local(): pl.pallas_call(kernel, in_specs=[pl.BlockSpec(memory_space=pltpu.SMEM), a...  96 us
    unnamed x2, local copies, waits for them, and re-layouts  2.64 us

profile of v3, /device:TPU:1, one launch (start us, length us, event | category | flops | bytes accessed | tf_op | source)
XLA Modules:
  0.0 99.3 jit_solution(3359704109638145608)
XLA Ops:
  0.6 96.0 %gradient_step.1 = (f32[2,4,256,256]{3,2,1,0:T(8,128)S(1)}, f32[2,4,256,256]{3,2,1,0:T(8,128)S(1)}) custom-call(s32[1,1,2,4]{3,2,1,0:T(2,128)} %bitcast.1, f32[2,4,256,256]{3,2,1,0:T(8,128)} %obj_any.1, f32[2,4,256,256]{3,2,1,0:T(8,128)} %probe_any.1, f32[4,1,1,4,256,256]{5,4,3,2,1,0:T(8,128)} %amp_any.1, f32[2,2,32,32]{3,2,1,0:T(8,128)} %kk.1, ...), custom_call_target="tpu_custom_call" | custom-call | tf_op jit(solution)/shard_map/gradient_step/pallas_call | solution.py:629
  96.7 1.3 %copy.11 = f32[2,4,256,256]{3,2,1,0:T(8,128)} copy(f32[2,4,256,256]{3,2,1,0:T(8,128)S(1)} %get-tuple-element.2) | data formatting | bytes 4194304
  98.0 1.3 %copy.12 = f32[2,4,256,256]{3,2,1,0:T(8,128)} copy(f32[2,4,256,256]{3,2,1,0:T(8,128)S(1)} %get-tuple-element.3) | data formatting | bytes 4194304
